TPU v7x, 32 devices: a whole 2x2x4 slice. The times are simulated.
32 devices in a mesh: comp: 2 (over y), lat: 4 (over x, core), lon: 4 (over z).
Axes of the slice: x: 2, y: 2, z: 4, core: 2. Of those that a mesh axis runs over, the one named last changes fastest.
Arguments:
- state: float32 [2, 3, 32, 64, 512], P('comp', None, None, 'lat', 'lon'), may hold values from -6 to 6
- wave_push: float32 [2, 32], P('comp'), may hold values from 0.2 to 0.6
- wave_fill: float32 [2, 32], P('comp'), may hold values from 0.2 to 0.6
- vertical: float32 [2, 32, 32], P('comp'), may hold values from -0.5 to 1
- land_mask: int32 [64, 512], P('lat', 'lon'), may hold values 0 or 1
- tile_match: int32 [4, 4, 2], P('lat'), may hold values from 0 to 3, as said below
- cell_counts: int32 [4, 4, 2], P('lat'), may hold values from 16 to 2032, as said below
Outputs:
- advanced: float32 [2, 3, 32, 64, 512], P('comp', None, None, 'lat', 'lon')
Inputs may be any that keep to these rules, and one draw needn't show every extreme that they name: tile_match(i, j, 0) = j, and tile_match(i, j, 1) is j - 1 or j + 1 taken modulo 4. cell_counts(i, j, 0) + cell_counts(i, j, 1) = 2048, with both entries positive multiples of 16.
All inputs are finite; a program needn't handle non-finite values. No bound on the sum of `land_mask` on one device may be relied on, other than what follows from the above.
Results may differ from a plain program's by a relative error of at most 0.0001.
Values sent between devices are 32-bit elements; how exact they have to be, the bound alone decides.
A program may use at most 64 MiB of HBM per device.

v0:
```python
import math

import jax
import jax.numpy as jnp
from jax import lax
from jax.sharding import PartitionSpec as P

KAPPA = 0.5
CORIOLIS = 0.4


def passed_along(array, axis, by):
    peers = lax.axis_size(axis)
    return lax.ppermute(array, axis, [(i, (i + by) % peers) for i in range(peers)])


def partner(block, axis, bit):
    count = lax.axis_size(axis)
    route = []
    for low in range(count):
        high = low | 1 << bit
        if high != low and high < count:
            route += [(low, high), (high, low)]
    return lax.ppermute(block, axis, route)


def extended_2(block, sides, width):
    for axis, dim in sides:
        count = lax.axis_size(axis)
        forward = [(i, i + 1) for i in range(count - 1)]
        forward.append((count - 1, 0))
        backward = [(target, source) for source, target in forward]
        low = lax.ppermute(
            lax.slice_in_dim(block, block.shape[dim] - width, None, axis=dim), axis, forward
        )
        high = lax.ppermute(lax.slice_in_dim(block, 0, width, axis=dim), axis, backward)
        block = jnp.concatenate([low, block, high], axis=dim)
    return block


def row_info(lat_id, rows, total_rows, width):
    global_rows = lat_id * rows + jnp.arange(rows + 2 * width) - width
    valid = ((global_rows >= 0) & (global_rows < total_rows)).astype(jnp.float32)
    angle = (global_rows.astype(jnp.float32) + 0.5) / total_rows - 0.5
    return (valid, CORIOLIS * jnp.sin(math.pi * angle))


def advance(extended, push, fill, vert, valid, fcor, mask_out):
    u_old, v_old, p_old = (extended[0], extended[1], extended[2])
    grad_x = (p_old[:, 1:-1, 2:] - p_old[:, 1:-1, :-2]) * 0.5
    grad_y = (p_old[:, 2:, 1:-1] - p_old[:, :-2, 1:-1]) * 0.5
    u_mid = u_old[:, 1:-1, 1:-1]
    v_mid = v_old[:, 1:-1, 1:-1]
    rot = fcor[1:-1][None, :, None]
    inside = valid[1:-1][None, :, None]
    u_one = (u_mid - push * grad_x + rot * v_mid) * inside
    v_one = (v_mid - push * grad_y - rot * u_mid) * inside
    div = (u_one[:, 1:-1, 2:] - u_one[:, 1:-1, :-2]) * 0.5 + (
        v_one[:, 2:, 1:-1] - v_one[:, :-2, 1:-1]
    ) * 0.5
    p_one = p_old[:, 2:-2, 2:-2] - fill * div
    p_two = jnp.einsum("am,myx->ayx", vert, p_one, precision=lax.Precision.HIGHEST)
    keep = (mask_out * valid[2:-2][:, None])[None]
    return jnp.stack([u_one[:, 1:-1, 1:-1] * keep, v_one[:, 1:-1, 1:-1] * keep, p_two * keep])


def tile_coef(pick_own, match_all, weight_all, lon_id, peer_id):
    match_own = lax.dynamic_index_in_dim(match_all, lon_id, 0, keepdims=False)
    weight_own = lax.dynamic_index_in_dim(weight_all, lon_id, 0, keepdims=False)
    match_peer = lax.dynamic_index_in_dim(match_all, peer_id, 0, keepdims=False)
    weight_peer = lax.dynamic_index_in_dim(weight_all, peer_id, 0, keepdims=False)
    own_coef = jnp.sum(weight_own * (match_own == peer_id).astype(jnp.float32))
    peer_coef = jnp.sum(weight_peer * (match_peer == lon_id).astype(jnp.float32))
    return jnp.where(pick_own, own_coef, peer_coef)


def remap_row(pick_own, center, match_all, weight_all, lon_id, n_lon):
    coef = tile_coef(pick_own, match_all, weight_all, lon_id, lon_id)
    total = coef * center
    weights = coef
    for offset in (1, -1):
        piece = passed_along(center, "lon", offset)
        peer_id = (lon_id - offset) % n_lon
        coef = tile_coef(pick_own, match_all, weight_all, lon_id, peer_id)
        total = total + coef * piece
        weights = weights + coef
    return total / weights


def shards(state, wave_push, wave_fill, vertical, land_mask, tile_match, cell_counts):
    fields = state[0]
    rows, cols = (fields.shape[2], fields.shape[3])
    comp_id = lax.axis_index("comp")
    lat_id = lax.axis_index("lat")
    lon_id = lax.axis_index("lon")
    n_lon = lax.axis_size("lon")
    total_rows = rows * lax.axis_size("lat")
    push = wave_push[0][:, None, None]
    fill = wave_fill[0][:, None, None]
    vert = vertical[0]
    ocean = comp_id == 1
    mask_local = jnp.where(
        ocean, land_mask.astype(jnp.float32), jnp.ones((rows, cols), jnp.float32)
    )
    surface = fields[:, 0]
    match_all = tile_match[0]
    weight_all = cell_counts[0].astype(jnp.float32)
    other = partner(surface, "comp", 0)
    remapped = remap_row(ocean, other, match_all, weight_all, lon_id, n_lon)
    valid, fcor = row_info(lat_id, rows, total_rows, 2)
    current = fields
    for step in range(2):
        extended = extended_2(current, (("lat", 2), ("lon", 3)), 2)
        extended = extended * valid[None, None, :, None]
        current = advance(extended, push, fill, vert, valid, fcor, mask_local)
    flux = KAPPA * (remapped - surface) * mask_local[None]
    top = current[:, 0] + flux
    result = jnp.concatenate([top[:, None], current[:, 1:]], axis=1)
    return result[None]


def solution(mesh):
    return jax.shard_map(
        shards,
        mesh=mesh,
        in_specs=(
            P("comp", None, None, "lat", "lon"),
            P("comp", None),
            P("comp", None),
            P("comp", None, None),
            P("lat", "lon"),
            P("lat", None, None),
            P("lat", None, None),
        ),
        out_specs=P("comp", None, None, "lat", "lon"),
        check_vma=False,
    )
```

profile of v0, /device:TPU:0, one launch (start us, length us, event | category | flops | bytes accessed | tf_op | source)
XLA Modules:
  0.0 48.3 jit_solution(4055700525462529315)
XLA Ops:
  0.0 1.2 %copy.119 = f32[1,3,32,16,128]{4,3,1,2,0:T(8,128)S(1)} copy(f32[1,3,32,16,128]{4,3,2,1,0:T(8,128)} %param.7) | data formatting | bytes 1572864 | tf_op args[0]
  1.2 0.1 fusion.50
  1.3 0.5 %collective-permute-start = (f32[3,32,2,128]{3,2,0,1:T(2,128)S(1)}, f32[3,32,2,128]{3,2,0,1:T(2,128)S(1)}, u32[]{:S(2)}, u32[]{:S(2)}) collective-permute-start(f32[3,32,2,128]{3,2,0,1:T(2,128)S(1)} %get-tuple-element.29), channel_id=1, source_target_pairs={{0,4},{4,8},{8,12},{12,0},{1,5},{5,9},{9,13},{13,1},{2,6},{6,10},{... | collective-permute-start | bytes 294920 | tf_op jit(solution)/shard_map/ppermute | solution.py:33
  1.9 2.0 %collective-permute-start.1 = (f32[3,32,2,128]{3,2,0,1:T(2,128)S(1)}, f32[3,32,2,128]{3,2,0,1:T(2,128)S(1)}, u32[]{:S(2)}, u32[]{:S(2)}) collective-permute-start(f32[3,32,2,128]{3,2,0,1:T(2,128)S(1)} %get-tuple-element.30), channel_id=1, source_target_pairs={{4,0},{8,4},{12,8},{0,12},{5,1},{9,5},{13,9},{1,13},{6,2},{10,6},{... | collective-permute-start | bytes 294920 | tf_op jit(solution)/shard_map/ppermute | solution.py:36
  3.9 0.1 slice.155
  3.9 0.1 fusion.40
  4.0 2.1 %collective-permute-done = f32[3,32,2,128]{3,2,0,1:T(2,128)S(1)} collective-permute-done((f32[3,32,2,128]{3,2,0,1:T(2,128)S(1)}, f32[3,32,2,128]{3,2,0,1:T(2,128)S(1)}, u32[]{:S(2)}, u32[]{:S(2)}) %collective-permute-start) | collective-permute-done | bytes 98336 | tf_op jit(solution)/shard_map/ppermute | solution.py:33
  6.1 0.9 %collective-permute-done.1 = f32[3,32,2,128]{3,2,0,1:T(2,128)S(1)} collective-permute-done((f32[3,32,2,128]{3,2,0,1:T(2,128)S(1)}, f32[3,32,2,128]{3,2,0,1:T(2,128)S(1)}, u32[]{:S(2)}, u32[]{:S(2)}) %collective-permute-start.1) | collective-permute-done | bytes 98336 | tf_op jit(solution)/shard_map/ppermute | solution.py:36
  7.0 0.2 pad_maximum_fusion.1
  7.2 0.4 fusion.48
  7.5 0.5 copy.61
  8.0 1.6 %collective-permute-start.2 = (f32[3,32,20,2]{1,3,2,0:T(2,128)S(1)}, f32[3,32,20,2]{1,3,2,0:T(2,128)S(1)}, u32[]{:S(2)}, u32[]{:S(2)}) collective-permute-start(f32[3,32,20,2]{1,3,2,0:T(2,128)S(1)} %copy.61), channel_id=1, source_target_pairs={{0,1},{1,2},{2,3},{3,0},{4,5},{5,6},{6,7},{7,4},{8,9},{9,10},{10,1... | collective-permute-start | bytes 46088 | tf_op jit(solution)/shard_map/ppermute | solution.py:33
  9.6 0.5 copy.62
  10.1 2.3 %collective-permute-start.3 = (f32[3,32,20,2]{1,3,2,0:T(2,128)S(1)}, f32[3,32,20,2]{1,3,2,0:T(2,128)S(1)}, u32[]{:S(2)}, u32[]{:S(2)}) collective-permute-start(f32[3,32,20,2]{1,3,2,0:T(2,128)S(1)} %copy.62), channel_id=1, source_target_pairs={{1,0},{2,1},{3,2},{0,3},{5,4},{6,5},{7,6},{4,7},{9,8},{10,9},{11,1... | collective-permute-start | bytes 46088 | tf_op jit(solution)/shard_map/ppermute | solution.py:36
  12.4 0.1 slice.153
  12.5 0.1 slice.150
  12.5 1.6 %collective-permute-done.2 = f32[3,32,20,2]{1,3,2,0:T(2,128)S(1)} collective-permute-done((f32[3,32,20,2]{1,3,2,0:T(2,128)S(1)}, f32[3,32,20,2]{1,3,2,0:T(2,128)S(1)}, u32[]{:S(2)}, u32[]{:S(2)}) %collective-permute-start.2) | collective-permute-done | bytes 15392 | tf_op jit(solution)/shard_map/ppermute | solution.py:33
  14.1 0.5 %copy.63 = f32[3,32,20,2]{3,2,0,1:T(8,128)S(1)} copy(f32[3,32,20,2]{1,3,2,0:T(2,128)S(1)} %collective-permute-done.2) | data formatting | bytes 30720 | tf_op jit(solution)/shard_map/ppermute | solution.py:33
  14.6 1.4 %collective-permute-done.3 = f32[3,32,20,2]{1,3,2,0:T(2,128)S(1)} collective-permute-done((f32[3,32,20,2]{1,3,2,0:T(2,128)S(1)}, f32[3,32,20,2]{1,3,2,0:T(2,128)S(1)}, u32[]{:S(2)}, u32[]{:S(2)}) %collective-permute-start.3) | collective-permute-done | bytes 15392 | tf_op jit(solution)/shard_map/ppermute | solution.py:36
  16.0 0.5 %copy.64 = f32[3,32,20,2]{3,2,0,1:T(8,128)S(1)} copy(f32[3,32,20,2]{1,3,2,0:T(2,128)S(1)} %collective-permute-done.3) | data formatting | bytes 30720 | tf_op jit(solution)/shard_map/ppermute | solution.py:36
  16.5 1.4 %maximum_multiply_fusion = f32[3,32,20,132]{3,2,0,1:T(8,128)S(1)} fusion(f32[3,32,20,2]{3,2,0,1:T(8,128)S(1)} %copy.64, f32[3,32,2,128]{3,2,0,1:T(2,128)S(1)} %collective-permute-done.1, f32[3,32,16,128]{3,2,0,1:T(8,128)S(1)} %bitcast.58, f32[3,32,2,128]{3,2,0,1:T(2,128)S(1)} %collective-permute-done, f32[3,32,20,2]{3,2,0,1:T(8,128)S(1)} %copy.63, ...), kind=kLoop, calls=%fused_computation | loop fusion | flops 1267200 | bytes 2027600 | tf_op jit(solution)/shard_map/mul | solution.py:114
  18.0 0.2 slice_bitcast_fusion.2
  18.2 1.1 %fusion.9 = (f32[32,18,130]{2,1,0:T(8,128)S(1)}, f32[32,18,130]{2,1,0:T(8,128)S(1)}) fusion(f32[32,20,132]{2,1,0:T(8,128)S(1)} %get-tuple-element.14, f32[32,20,132]{2,1,0:T(8,128)S(1)} %get-tuple-element.13, f32[32,20,132]{2,1,0:T(8,128)S(1)} %get-tuple-element.12, f32[32]{0:T(128)S(1)} %multiply_bitcast_fusion.1, f32[18]{0:T(128)S(1)} %slice.153, ...), kind=kLoop, calls=%fused_computation.20 | loop fusion | flops 898560 | bytes 2396432 | tf_op jit(solution)/shard_map/mul | solution.py:56
  19.4 0.5 %fusion.31 = (f32[1,32,16,128]{3,2,1,0:T(8,128)S(1)}, f32[32,16,128]{2,1,0:T(8,128)S(1)}, f32[1,32,16,128]{3,2,1,0:T(8,128)S(1)}) fusion(f32[32,18,130]{2,1,0:T(8,128)S(1)} %get-tuple-element.10, f32[16,128]{1,0:T(8,128)S(1)} %get-tuple-element.34, f32[32]{0:T(128)S(1)} %multiply_bitcast_fusion, f32[32,18,130]{2,1,0:T(8,128)S(1)} %get-tuple-element.11, ...), kind=kLoop, calls=%fused_computation.58 | loop fusion | flops 458752 | bytes 2629760 | tf_op jit(solution)/shard_map/stack | solution.py:64
  19.9 0.5 fusion.35
  20.4 0.2 fusion.34
  20.5 0.0 copy-start.2
  20.6 0.1 pad_maximum_fusion.5
  20.6 0.2 collective-permute-start.4
  20.8 1.6 %collective-permute-start.5 = (f32[3,32,2,128]{3,2,1,0:T(2,128)S(1)}, f32[3,32,2,128]{3,2,1,0:T(2,128)S(1)}, u32[]{:S(2)}, u32[]{:S(2)}) collective-permute-start(f32[3,32,2,128]{3,2,1,0:T(2,128)S(1)} %get-tuple-element.25), channel_id=1, source_target_pairs={{4,0},{8,4},{12,8},{0,12},{5,1},{9,5},{13,9},{1,13},{6,2},{10,6},{... | collective-permute-start | bytes 294920 | tf_op jit(solution)/shard_map/ppermute | solution.py:36
  22.4 0.6 %slice_bitcast_fusion.5 = f32[3,16,128]{2,1,0:T(8,128)} fusion(f32[3,32,16,128]{3,2,0,1:T(8,128)S(1)} %bitcast.59), kind=kLoop, calls=%fused_computation.71 | loop fusion | bytes 49152 | tf_op jit(solution)/shard_map/squeeze | solution.py:105
  23.0 1.5 %collective-permute-start.8 = (f32[3,16,128]{2,1,0:T(8,128)}, f32[3,16,128]{2,1,0:T(8,128)}, u32[]{:S(2)}, u32[]{:S(2)}) collective-permute-start(f32[3,16,128]{2,1,0:T(8,128)} %slice_bitcast_fusion.5), channel_id=1, source_target_pairs={{0,16},{16,0},{1,17},{17,1},{2,18},{18,2},{3,19},{19,3},{4,20},{20... | collective-permute-start | bytes 73736 | tf_op jit(solution)/shard_map/ppermute | solution.py:24
  24.6 0.2 collective-permute-done.4
  24.7 0.2 pad_maximum_fusion.2
  25.0 0.4 fusion.47
  25.3 0.0 copy-done.3
  25.4 1.1 %copy.72 = f32[3,32,20,2]{1,3,2,0:T(2,128)} copy(f32[3,32,20,2]{3,2,1,0:T(8,128)S(1)} %get-tuple-element.18) | data formatting | bytes 30720 | tf_op jit(solution)/shard_map/slice | solution.py:34
  26.4 0.8 %collective-permute-start.6 = (f32[3,32,20,2]{1,3,2,0:T(2,128)}, f32[3,32,20,2]{1,3,2,0:T(2,128)S(1)}, u32[]{:S(2)}, u32[]{:S(2)}) collective-permute-start(f32[3,32,20,2]{1,3,2,0:T(2,128)} %copy.72), channel_id=1, source_target_pairs={{0,1},{1,2},{2,3},{3,0},{4,5},{5,6},{6,7},{7,4},{8,9},{9,10},{10,1... | collective-permute-start | bytes 46088 | tf_op jit(solution)/shard_map/ppermute | solution.py:33
  27.3 0.5 copy.73
  27.7 3.0 %collective-permute-start.7 = (f32[3,32,20,2]{1,3,2,0:T(2,128)S(1)}, f32[3,32,20,2]{1,3,2,0:T(2,128)}, u32[]{:S(2)}, u32[]{:S(2)}) collective-permute-start(f32[3,32,20,2]{1,3,2,0:T(2,128)S(1)} %copy.73), channel_id=1, source_target_pairs={{1,0},{2,1},{3,2},{0,3},{5,4},{6,5},{7,6},{4,7},{9,8},{10,9},{11,1... | collective-permute-start | bytes 46088 | tf_op jit(solution)/shard_map/ppermute | solution.py:36
  30.8 0.8 %fusion.46 = (f32[]{:T(128)}, f32[]{:T(128)}, f32[]{:T(128)}, f32[]{:T(128)}, f32[]{:T(128)}) fusion(f32[1,4,2]{1,2,0:T(2,128)S(1)} %convert_element_type.26, s32[]{:T(128)S(6)} %select_n.54, s32[1,4,2]{1,2,0:T(2,128)S(1)} %copy-done.4, s32[]{:T(128)S(6)} %axis_index.38, s32[]{:T(128)S(6)} %select_n.49, s32[]{:T(128)S(6)} %select_n.50, s32[]{:T(128)S(6)} %select_n.53, ...), kind=kLoop, calls=%fused_computation.95 | loop fusion | flops 25 | bytes 92 | tf_op jit(solution)/shard_map/reduce_sum | solution.py:73
  34.6 1.6 %collective-permute-start.10 = (f32[3,16,128]{2,1,0:T(8,128)}, f32[3,16,128]{2,1,0:T(8,128)}, u32[]{:S(2)}, u32[]{:S(2)}) collective-permute-start(f32[3,16,128]{2,1,0:T(8,128)} %collective-permute-done.8), channel_id=1, source_target_pairs={{0,3},{1,0},{2,1},{3,2},{4,7},{5,4},{6,5},{7,6},{8,11},{9,8},{10,9... | collective-permute-start | bytes 73736 | tf_op jit(solution)/shard_map/ppermute | solution.py:14
  36.2 0.5 %collective-permute-start.9 = (f32[3,16,128]{2,1,0:T(8,128)}, f32[3,16,128]{2,1,0:T(8,128)}, u32[]{:S(2)}, u32[]{:S(2)}) collective-permute-start(f32[3,16,128]{2,1,0:T(8,128)} %collective-permute-done.8), channel_id=1, source_target_pairs={{0,1},{1,2},{2,3},{3,0},{4,5},{5,6},{6,7},{7,4},{8,9},{9,10},{10,1... | collective-permute-start | bytes 73736 | tf_op jit(solution)/shard_map/ppermute | solution.py:14
  36.7 0.5 %copy.74 = f32[3,32,20,2]{3,2,1,0:T(8,128)S(1)} copy(f32[3,32,20,2]{1,3,2,0:T(2,128)S(1)} %collective-permute-done.6) | data formatting | bytes 30720 | tf_op jit(solution)/shard_map/ppermute | solution.py:33
  37.2 1.3 %copy.75 = f32[3,32,20,2]{3,2,1,0:T(8,128)S(1)} copy(f32[3,32,20,2]{1,3,2,0:T(2,128)} %collective-permute-done.7) | data formatting | bytes 30720 | tf_op jit(solution)/shard_map/ppermute | solution.py:36
  38.5 2.5 %pad_maximum_fusion = f32[3,32,20,132]{3,2,1,0:T(8,128)S(1)} fusion(f32[3,32,20,2]{3,2,1,0:T(8,128)S(1)} %copy.75, f32[3,32,2,128]{3,2,1,0:T(2,128)} %copy-done.3, f32[1,32,16,128]{3,2,1,0:T(8,128)} %copy-done.2, f32[1,32,16,128]{3,2,1,0:T(8,128)} %copy-done.1, f32[1,32,16,128]{3,2,1,0:T(8,128)S(1)} %get-tuple-element.26, ...), kind=kLoop, calls=%fused_computation.1 | loop fusion | flops 1520640 | bytes 2027520 | tf_op jit(solution)/shard_map/concatenate | solution.py:37
  41.0 0.6 %copy_multiply_fusion = f32[3,32,20,132]{3,1,2,0:T(8,128)S(1)} fusion(f32[3,32,20,132]{3,2,1,0:T(8,128)S(1)} %pad_maximum_fusion, f32[20]{0:T(128)S(1)} %and_convert_fusion), kind=kLoop, calls=%fused_computation.2 | loop fusion | flops 253440 | bytes 2027600 | tf_op jit(solution)/shard_map/mul | solution.py:114
  41.6 0.2 slice_bitcast_fusion.3
  41.8 0.4 copy.118
  42.2 0.2 slice.215
  42.5 0.0 copy-done.9
  42.5 0.5 %fusion.49 = (f32[32,18,130]{2,1,0:T(8,128)S(1)}, f32[32,18,130]{2,1,0:T(8,128)S(1)}, f32[32,18,130]{2,1,0:T(8,128)S(1)}) fusion(f32[32,20,132]{2,1,0:T(8,128)S(1)} %bitcast.61, f32[18]{0:T(128)S(1)} %copy-done.9, f32[32,18,130]{2,0,1:T(8,128)S(1)} %slice.215), kind=kLoop, calls=%fused_computation.102 | loop fusion | flops 149760 | bytes 1497672 | tf_op jit(solution)/shard_map/slice | solution.py:52
  43.0 0.1 copy-done.7
  43.1 0.7 %fusion.17 = (f32[32,18,130]{2,0,1:T(8,128)S(1)}, f32[32,18,130]{2,0,1:T(8,128)S(1)}) fusion(f32[32,20,132]{2,0,1:T(8,128)S(1)} %get-tuple-element.16, f32[32,18,130]{2,1,0:T(8,128)S(1)} %get-tuple-element.35, f32[32,18,130]{2,1,0:T(8,128)S(1)} %get-tuple-element.22, f32[18]{0:T(128)S(1)} %copy-done.7, f32[32]{0:T(128)S(1)} %multiply_bitcast_fusion.1, ...), kind=kLoop, calls=%fused_computation.37 | loop fusion | flops 748800 | bytes 2995400 | tf_op jit(solution)/shard_map/mul | solution.py:56
  43.9 0.1 slice.219
  44.0 0.7 %fusion.21 = f32[16,128,32]{1,2,0:T(8,128)S(1)} fusion(f32[32,18,130]{2,0,1:T(8,128)S(1)} %get-tuple-element.32, f32[32,18,130]{2,0,1:T(8,128)S(1)} %get-tuple-element.31, f32[32,20,132]{2,0,1:T(8,128)S(1)} %get-tuple-element.16, f32[32]{0:T(128)S(1)} %multiply_bitcast_fusion, f32[1,32,32]{2,1,0:T(8,128)S(1)} %copy-done), kind=kOutput, calls=%fused_computation.43 | convolution fusion | flops 25493504 | bytes 1589760 | tf_op jit(solution)/shard_map/am,myx->ayx/dot_general | solution.py:62
  44.7 0.1 fusion.26
  44.9 0.2 fusion.32
  45.0 0.1 copy.88
  45.1 0.2 fusion.33
  45.3 0.1 copy.89
  45.4 1.5 %multiply_add_fusion = f32[3,16,128]{2,1,0:T(8,128)S(1)} fusion(f32[3,16,128]{2,1,0:T(8,128)S(1)} %bitcast.62, f32[3,16,128]{2,1,0:T(8,128)} %collective-permute-done.10, f32[3,16,128]{2,1,0:T(8,128)} %collective-permute-done.9, f32[3,16,128]{2,1,0:T(8,128)} %collective-permute-done.8, f32[16,128]{1,0:T(8,128)S(1)} %get-tuple-element.33, f32[]{:T(128)S(6)} %add.86, ...), kind=kLoop, calls=%fused_computation.73 | loop fusion | flops 55296 | bytes 155664 | tf_op jit(solution)/shard_map/add | solution.py:117
  46.9 0.1 fusion.1
  47.0 1.3 %copy.91 = f32[1,3,32,16,128]{4,3,2,1,0:T(8,128)} copy(f32[1,3,32,16,128]{4,2,3,1,0:T(8,128)S(1)} %fusion.1) | data formatting | bytes 1572864 | tf_op jit(solution)/shard_map/broadcast_in_dim | solution.py:119
  (34 shorter events, 0.1 us)
Async XLA Ops:
  0.0 19.9 %copy-start = (f32[1,32,32]{2,1,0:T(8,128)S(1)}, f32[1,32,32]{2,1,0:T(8,128)}, u32[]{:S(2)}) copy-start(f32[1,32,32]{2,1,0:T(8,128)} %param.10) | copy-start | bytes 12292
  0.0 3.9 %copy-start.11 = (f32[1,32]{1,0:T(1,128)S(1)}, f32[1,32]{1,0:T(1,128)}, u32[]{:S(2)}) copy-start(f32[1,32]{1,0:T(1,128)} %param.8) | copy-start | bytes 388
  0.0 3.9 %copy-start.5 = (s32[16,128]{1,0:T(8,128)S(1)}, s32[16,128]{1,0:T(8,128)}, u32[]{:S(2)}) copy-start(s32[16,128]{1,0:T(8,128)} %param.11) | copy-start | bytes 24580
  0.0 4.0 %copy-start.12 = (f32[1,32]{1,0:T(1,128)S(1)}, f32[1,32]{1,0:T(1,128)}, u32[]{:S(2)}) copy-start(f32[1,32]{1,0:T(1,128)} %param.9) | copy-start | bytes 388
  1.3 4.8 %collective-permute-start = (f32[3,32,2,128]{3,2,0,1:T(2,128)S(1)}, f32[3,32,2,128]{3,2,0,1:T(2,128)S(1)}, u32[]{:S(2)}, u32[]{:S(2)}) collective-permute-start(f32[3,32,2,128]{3,2,0,1:T(2,128)S(1)} %get-tuple-element.29), channel_id=1, source_target_pairs={{0,4},{4,8},{8,12},{12,0},{1,5},{5,9},{9,13},{13,1},{2,6},{6,10},{... | collective-permute-start | bytes 294920 | tf_op jit(solution)/shard_map/ppermute | solution.py:33
  1.9 5.1 %collective-permute-start.1 = (f32[3,32,2,128]{3,2,0,1:T(2,128)S(1)}, f32[3,32,2,128]{3,2,0,1:T(2,128)S(1)}, u32[]{:S(2)}, u32[]{:S(2)}) collective-permute-start(f32[3,32,2,128]{3,2,0,1:T(2,128)S(1)} %get-tuple-element.30), channel_id=1, source_target_pairs={{4,0},{8,4},{12,8},{0,12},{5,1},{9,5},{13,9},{1,13},{6,2},{10,6},{... | collective-permute-start | bytes 294920 | tf_op jit(solution)/shard_map/ppermute | solution.py:36
  8.0 6.1 %collective-permute-start.2 = (f32[3,32,20,2]{1,3,2,0:T(2,128)S(1)}, f32[3,32,20,2]{1,3,2,0:T(2,128)S(1)}, u32[]{:S(2)}, u32[]{:S(2)}) collective-permute-start(f32[3,32,20,2]{1,3,2,0:T(2,128)S(1)} %copy.61), channel_id=1, source_target_pairs={{0,1},{1,2},{2,3},{3,0},{4,5},{5,6},{6,7},{7,4},{8,9},{9,10},{10,1... | collective-permute-start | bytes 46088 | tf_op jit(solution)/shard_map/ppermute | solution.py:33
  10.1 5.9 %collective-permute-start.3 = (f32[3,32,20,2]{1,3,2,0:T(2,128)S(1)}, f32[3,32,20,2]{1,3,2,0:T(2,128)S(1)}, u32[]{:S(2)}, u32[]{:S(2)}) collective-permute-start(f32[3,32,20,2]{1,3,2,0:T(2,128)S(1)} %copy.62), channel_id=1, source_target_pairs={{1,0},{2,1},{3,2},{0,3},{5,4},{6,5},{7,6},{4,7},{9,8},{10,9},{11,1... | collective-permute-start | bytes 46088 | tf_op jit(solution)/shard_map/ppermute | solution.py:36
  12.5 5.7 %copy-start.6 = (f32[18]{0:T(128)}, f32[18]{0:T(128)S(1)}, u32[]{:S(2)}) copy-start(f32[18]{0:T(128)S(1)} %slice.153) | copy-start | bytes 220
  12.5 5.7 %copy-start.8 = (f32[18]{0:T(128)}, f32[18]{0:T(128)S(1)}, u32[]{:S(2)}) copy-start(f32[18]{0:T(128)S(1)} %slice.150) | copy-start | bytes 220
  19.9 5.1 %copy-start.1 = (f32[1,32,16,128]{3,2,1,0:T(8,128)}, f32[1,32,16,128]{3,2,1,0:T(8,128)S(1)}, u32[]{:S(2)}) copy-start(f32[1,32,16,128]{3,2,1,0:T(8,128)S(1)} %get-tuple-element.28) | copy-start | bytes 786436
  20.5 4.4 %copy-start.2 = (f32[1,32,16,128]{3,2,1,0:T(8,128)}, f32[1,32,16,128]{3,2,1,0:T(8,128)S(1)}, u32[]{:S(2)}) copy-start(f32[1,32,16,128]{3,2,1,0:T(8,128)S(1)} %fusion.34) | copy-start | bytes 786436
  20.6 4.1 %collective-permute-start.4 = (f32[3,32,2,128]{3,2,1,0:T(2,128)S(1)}, f32[3,32,2,128]{3,2,1,0:T(2,128)S(1)}, u32[]{:S(2)}, u32[]{:S(2)}) collective-permute-start(f32[3,32,2,128]{3,2,1,0:T(2,128)S(1)} %get-tuple-element.24), channel_id=1, source_target_pairs={{0,4},{4,8},{8,12},{12,0},{1,5},{5,9},{9,13},{13,1},{2,6},{6,10},{... | collective-permute-start | bytes 294920 | tf_op jit(solution)/shard_map/ppermute | solution.py:33
  20.8 3.9 %collective-permute-start.5 = (f32[3,32,2,128]{3,2,1,0:T(2,128)S(1)}, f32[3,32,2,128]{3,2,1,0:T(2,128)S(1)}, u32[]{:S(2)}, u32[]{:S(2)}) collective-permute-start(f32[3,32,2,128]{3,2,1,0:T(2,128)S(1)} %get-tuple-element.25), channel_id=1, source_target_pairs={{4,0},{8,4},{12,8},{0,12},{5,1},{9,5},{13,9},{1,13},{6,2},{10,6},{... | collective-permute-start | bytes 294920 | tf_op jit(solution)/shard_map/ppermute | solution.py:36
  23.0 11.5 %collective-permute-start.8 = (f32[3,16,128]{2,1,0:T(8,128)}, f32[3,16,128]{2,1,0:T(8,128)}, u32[]{:S(2)}, u32[]{:S(2)}) collective-permute-start(f32[3,16,128]{2,1,0:T(8,128)} %slice_bitcast_fusion.5), channel_id=1, source_target_pairs={{0,16},{16,0},{1,17},{17,1},{2,18},{18,2},{3,19},{19,3},{4,20},{20... | collective-permute-start | bytes 73736 | tf_op jit(solution)/shard_map/ppermute | solution.py:24
  24.7 0.6 %copy-start.3 = (f32[3,32,2,128]{3,2,1,0:T(2,128)}, f32[3,32,2,128]{3,2,1,0:T(2,128)S(1)}, u32[]{:S(2)}) copy-start(f32[3,32,2,128]{3,2,1,0:T(2,128)S(1)} %collective-permute-done.5) | copy-start | bytes 294916
  25.4 5.4 %copy-start.4 = (s32[1,4,2]{1,2,0:T(2,128)S(1)}, s32[1,4,2]{1,2,0:T(2,128)}, u32[]{:S(2)}) copy-start(s32[1,4,2]{1,2,0:T(2,128)} %param.12) | copy-start | bytes 100
  26.4 4.3 %copy-start.10 = (s32[1,4,2]{1,2,0:T(2,128)S(1)}, s32[1,4,2]{1,2,0:T(2,128)}, u32[]{:S(2)}) copy-start(s32[1,4,2]{1,2,0:T(2,128)} %param.13) | copy-start | bytes 100
  26.4 10.2 %collective-permute-start.6 = (f32[3,32,20,2]{1,3,2,0:T(2,128)}, f32[3,32,20,2]{1,3,2,0:T(2,128)S(1)}, u32[]{:S(2)}, u32[]{:S(2)}) collective-permute-start(f32[3,32,20,2]{1,3,2,0:T(2,128)} %copy.72), channel_id=1, source_target_pairs={{0,1},{1,2},{2,3},{3,0},{4,5},{5,6},{6,7},{7,4},{8,9},{9,10},{10,1... | collective-permute-start | bytes 46088 | tf_op jit(solution)/shard_map/ppermute | solution.py:33
  27.7 9.4 %collective-permute-start.7 = (f32[3,32,20,2]{1,3,2,0:T(2,128)S(1)}, f32[3,32,20,2]{1,3,2,0:T(2,128)}, u32[]{:S(2)}, u32[]{:S(2)}) collective-permute-start(f32[3,32,20,2]{1,3,2,0:T(2,128)S(1)} %copy.73), channel_id=1, source_target_pairs={{1,0},{2,1},{3,2},{0,3},{5,4},{6,5},{7,6},{4,7},{9,8},{10,9},{11,1... | collective-permute-start | bytes 46088 | tf_op jit(solution)/shard_map/ppermute | solution.py:36
  34.6 10.8 %collective-permute-start.10 = (f32[3,16,128]{2,1,0:T(8,128)}, f32[3,16,128]{2,1,0:T(8,128)}, u32[]{:S(2)}, u32[]{:S(2)}) collective-permute-start(f32[3,16,128]{2,1,0:T(8,128)} %collective-permute-done.8), channel_id=1, source_target_pairs={{0,3},{1,0},{2,1},{3,2},{4,7},{5,4},{6,5},{7,6},{8,11},{9,8},{10,9... | collective-permute-start | bytes 73736 | tf_op jit(solution)/shard_map/ppermute | solution.py:14
  36.2 9.3 %collective-permute-start.9 = (f32[3,16,128]{2,1,0:T(8,128)}, f32[3,16,128]{2,1,0:T(8,128)}, u32[]{:S(2)}, u32[]{:S(2)}) collective-permute-start(f32[3,16,128]{2,1,0:T(8,128)} %collective-permute-done.8), channel_id=1, source_target_pairs={{0,1},{1,2},{2,3},{3,0},{4,5},{5,6},{6,7},{7,4},{8,9},{9,10},{10,1... | collective-permute-start | bytes 73736 | tf_op jit(solution)/shard_map/ppermute | solution.py:14
  41.8 0.6 %copy-start.9 = (f32[18]{0:T(128)S(1)}, f32[18]{0:T(128)}, u32[]{:S(2)}) copy-start(f32[18]{0:T(128)} %copy-done.8) | copy-start | bytes 220
  42.5 0.7 %copy-start.7 = (f32[18]{0:T(128)S(1)}, f32[18]{0:T(128)}, u32[]{:S(2)}) copy-start(f32[18]{0:T(128)} %copy-done.6) | copy-start | bytes 220
where the time goes:
time: 48.7 us; the launch traced here: 48.3 us
  starting transfers between devices  15.7 us (32%)
  local copies, waits for them, and re-layouts  11 us (23%)
  other arithmetic  11 us (23%)
  waiting for transfers between devices  6.07 us (12%)
  between operations  3.4 us (7%)
  matrix products  1.16 us (2%)
    ppermute x4, starting transfers between devices, extended_2(): lax.ppermute(lax.slice_in_dim(block, 0, width, axis=dim), axis, backward)  8.9 us
    ppermute x4, waiting for transfers between devices, extended_2(): lax.ppermute(lax.slice_in_dim(block, block.shape[dim] - width, None, axis...  3.8 us
    ppermute x4, starting transfers between devices, extended_2(): lax.ppermute(lax.slice_in_dim(block, block.shape[dim] - width, None, axis...  3.15 us
    concatenate x3, other arithmetic, extended_2(): block = jnp.concatenate([low, block, high], axis=dim)  2.9 us
    slice x5, local copies, waits for them, and re-layouts, extended_2(): lax.slice_in_dim(block, block.shape[dim] - width, None, axis=dim)  2.33 us
    ppermute x4, waiting for transfers between devices, extended_2(): lax.ppermute(lax.slice_in_dim(block, 0, width, axis=dim), axis, backward)  2.26 us
    ppermute x2, starting transfers between devices, passed_along(): lax.ppermute(array, axis, [(i, (i + by) % peers) for i in range(peers)])  2.08 us
    mul x2, other arithmetic, shards(): extended = extended * valid[None, None, :, None]  2.06 us
  transfers between devices with their start and end apart: 11, of which 5 were waited for; matrix products, arithmetic and copies ran while one was open for 27% of the time, Pallas kernels for 0%

commit v1 on v0

v1 whole, which is shorter than its diff:
```python
import functools
import math

import jax
import jax.numpy as jnp
from jax import lax
from jax.experimental import pallas as pl
from jax.experimental.pallas import tpu as pltpu
from jax.sharding import PartitionSpec as P

KAPPA = 0.5
CORIOLIS = 0.4
MESH = pl.DeviceIdType.MESH
STEPS = 2


def kernel(
    sizes,
    state,
    push_in,
    fill_in,
    vert_in,
    land_in,
    match_in,
    count_in,
    out,
    raw,
    push_v,
    fill_v,
    vert_v,
    land_v,
    match_v,
    count_v,
    pres,
    uone,
    vone,
    pone,
    unew,
    vnew,
    pack,
    from_lo,
    from_hi,
    edge,
    row_lo,
    row_hi,
    surf,
    load_sem,
    send_sem,
    recv_sem,
):
    levels, rows, cols, n_lat, n_lon = sizes
    comp = lax.axis_index("comp")
    lat = lax.axis_index("lat")
    lon = lax.axis_index("lon")
    west = lax.rem(lon + n_lon - 1, n_lon)
    east = lax.rem(lon + 1, n_lon)
    south = lax.rem(lat + n_lat - 1, n_lat)
    north = lax.rem(lat + 1, n_lat)
    other = 1 - comp
    plane = levels * rows

    barrier = pltpu.get_barrier_semaphore()
    for to in (
        (comp, lat, west),
        (comp, lat, east),
        (comp, south, lon),
        (comp, north, lon),
        (other, lat, lon),
        (other, lat, west),
        (other, lat, east),
    ):
        pl.semaphore_signal(barrier, inc=1, device_id=to, device_id_type=MESH)

    loads = []
    for f in (2, 0, 1):
        loads.append(
            pltpu.make_async_copy(
                state.at[pl.ds(f * plane, plane)],
                raw.at[pl.ds(f * plane, plane)],
                load_sem.at[f],
            )
        )
    for k, (src, dst) in enumerate(
        (
            (push_in, push_v),
            (fill_in, fill_v),
            (vert_in, vert_v),
            (land_in, land_v),
            (match_in, match_v),
            (count_in, count_v),
        )
    ):
        loads.append(pltpu.make_async_copy(src, dst, load_sem.at[3 + k]))
    for copy in loads:
        copy.start()

    lane = lax.broadcasted_iota(jnp.int32, (levels, cols), 1)
    first = lane == 0
    last = lane == cols - 1
    quad = lax.rem(lane, 4)
    row_id = lax.broadcasted_iota(jnp.int32, (rows, cols), 0) + lat * rows
    angle = (row_id.astype(jnp.float32) + 0.5) / (n_lat * rows) - 0.5
    fcor = CORIOLIS * jnp.sin(math.pi * angle)
    has_south = (lat > 0).astype(jnp.float32)
    has_north = (lat < n_lat - 1).astype(jnp.float32)

    for copy in loads:
        copy.wait()

    diag = lax.broadcasted_iota(jnp.int32, (levels, levels), 0) == lax.broadcasted_iota(
        jnp.int32, (levels, levels), 1
    )

    def per_level(ref):
        wide = jnp.broadcast_to(ref[...], (levels, levels))
        column = jnp.sum(jnp.where(diag, wide, 0.0), axis=1, keepdims=True)
        return jnp.broadcast_to(column * 0.5, (levels, cols))

    hp = per_level(push_v)
    hf = per_level(fill_v)
    vert = vert_v[...]
    vert_hi = vert.astype(jnp.bfloat16).astype(jnp.float32)
    vert_cat = jnp.concatenate([vert_hi, vert_hi, vert - vert_hi], axis=1).astype(
        jnp.bfloat16
    )
    mask = jnp.where(comp == 1, land_v[...].astype(jnp.float32), 1.0)

    def level_rows(y):
        return pl.ds(y, levels, stride=rows)

    def back(x):
        return jnp.where(first, 0.0, pltpu.roll(x, 1, 1))

    def ahead(x):
        return jnp.where(last, 0.0, pltpu.roll(x, cols - 1, 1))

    def remote(src, dst, k, to):
        return pltpu.make_async_remote_copy(
            src_ref=src,
            dst_ref=dst,
            send_sem=send_sem.at[k],
            recv_sem=recv_sem.at[k],
            device_id=to,
            device_id_type=MESH,
        )

    sends = []
    surf_sends = []
    for step in range(STEPS):
        base = 3 + 4 * step

        def get(f, y):
            if step == 0:
                return raw[pl.ds(f * plane + y, levels, stride=rows), :]
            return (unew, vnew, pres)[f][y]

        packed = jnp.zeros((levels, cols), jnp.float32)
        for y in range(rows):
            p = get(2, y)
            if step == 0:
                pres[y] = p
            u1 = get(0, y) + fcor[y : y + 1] * get(1, y) - hp * (ahead(p) - back(p))
            uone[y] = u1
            at = 4 * y + 2
            here = (lane == at) | (lane == at - 1)
            packed = jnp.where(here, pltpu.roll(p, at, 1), packed)
            at = 4 * (rows + y) + 2
            here = (lane == at) | (lane == at - 1)
            packed = jnp.where(here, pltpu.roll(u1, at, 1), packed)
        pack[step] = packed
        for y in (0, rows - 1):
            v1 = get(1, y) - fcor[y : y + 1] * get(0, y)
            v1 = v1 - hp * pres[y + 1] if y == 0 else v1 + hp * pres[y - 1]
            vone[y] = v1
            k = 0 if y == 0 else 1
            edge[step, k, 0] = pres[y]
            edge[step, k, 1] = v1
        if step == 0:
            pl.semaphore_wait(barrier, 7)
        lo = remote(pack.at[step], from_lo.at[step], base, (comp, lat, east))
        hi = remote(pack.at[step], from_hi.at[step], base + 1, (comp, lat, west))
        down = remote(edge.at[step, 0], row_hi.at[step], base + 2, (comp, south, lon))
        up = remote(edge.at[step, 1], row_lo.at[step], base + 3, (comp, north, lon))
        for copy in (lo, hi, down, up):
            copy.start()
            sends.append(copy)
        if step == 0:
            for k, to in enumerate((lon, east, west)):
                for f in range(3):
                    copy = remote(
                        raw.at[pl.ds(f * plane, rows)],
                        surf.at[k, f],
                        3 + 4 * STEPS + 3 * k + f,
                        (other, lat, to),
                    )
                    copy.start()
                    surf_sends.append(copy)

        for y in range(1, rows - 1):
            vone[y] = (
                get(1, y) - fcor[y : y + 1] * get(0, y) - hp * (pres[y + 1] - pres[y - 1])
            )
        for y in range(rows):
            u1 = uone[y]
            div = ahead(u1) - back(u1)
            if y + 1 < rows:
                div = div + vone[y + 1]
            if y > 0:
                div = div - vone[y - 1]
            pone[y] = pres[y] - hf * div

        down.wait_recv()
        up.wait_recv()
        p_lo = has_south * row_lo[step, 0]
        p_hi = has_north * row_hi[step, 0]
        v_lo = has_south * (row_lo[step, 1] - hp * pres[0])
        v_hi = has_north * (row_hi[step, 1] + hp * pres[rows - 1])
        fix_lo = hp * p_lo
        fix_hi = -hp * p_hi
        vone[0] = vone[0] + fix_lo
        vone[rows - 1] = vone[rows - 1] + fix_hi
        pone[0] = pone[0] + hf * v_lo
        pone[1] = pone[1] + hf * fix_lo
        pone[rows - 1] = pone[rows - 1] - hf * v_hi
        pone[rows - 2] = pone[rows - 2] - hf * fix_hi

        lo.wait_recv()
        hi.wait_recv()
        moved = jnp.where(
            quad == 1,
            pltpu.roll(from_hi[step], cols - 1, 1),
            pltpu.roll(from_lo[step], 1, 1),
        )
        signed = jnp.where(quad == 1, hp, -hp)
        u_side = pltpu.roll(moved, cols - 4 * rows, 1) + signed * packed
        u_fix = -signed * moved
        d_fix = jnp.where(
            quad == 1,
            u_side,
            jnp.where(
                quad == 2,
                -u_side,
                jnp.where(
                    quad == 0, pltpu.roll(u_fix, cols - 1, 1), -pltpu.roll(u_fix, 1, 1)
                ),
            ),
        )
        d_fix = hf * d_fix
        ends = first | last
        near = (lane < 2) | (lane > cols - 3)
        pieces = []
        for y in range(rows):
            turn = cols - (4 * y + 2)
            uone[y] = uone[y] + jnp.where(ends, pltpu.roll(u_fix, turn, 1), 0.0)
            p1 = pone[y] - jnp.where(near, pltpu.roll(d_fix, turn, 1), 0.0)
            p1_hi = p1.astype(jnp.bfloat16)
            p1_lo = (p1 - p1_hi.astype(jnp.float32)).astype(jnp.bfloat16)
            pieces.append(jnp.concatenate([p1_hi, p1_lo, p1_hi], axis=0))
        p2 = jnp.dot(
            vert_cat, jnp.concatenate(pieces, axis=1), preferred_element_type=jnp.float32
        )
        for y in range(rows):
            keep = mask[y : y + 1]
            u2 = keep * uone[y]
            v2 = keep * vone[y]
            pn = keep * p2[:, y * cols : (y + 1) * cols]
            if step + 1 < STEPS:
                unew[y] = u2
                vnew[y] = v2
                pres[y] = pn
            else:
                for f, value in enumerate((u2, v2, pn)):
                    out[pl.ds(f * plane + y, levels, stride=rows), :] = value

    count = count_v[...].astype(jnp.float32)
    match = match_v[...]
    tile = lax.broadcasted_iota(jnp.int32, match.shape, 0)

    def coef(peer):
        own = jnp.where((tile == lon) & (match == peer), count, 0.0)
        theirs = jnp.where((tile == peer) & (match == lon), count, 0.0)
        picked = jnp.where(comp == 1, own, theirs)
        total = jnp.sum(jnp.sum(picked, axis=1, keepdims=True), axis=0, keepdims=True)
        return jnp.broadcast_to(total, (rows, cols))

    coefs = [coef(lon), coef(west), coef(east)]
    inverse = KAPPA * mask / (coefs[0] + coefs[1] + coefs[2])
    scaled = [c * inverse for c in coefs]
    for copy in surf_sends:
        copy.wait_recv()
    for f in range(3):
        at = pl.ds(f * plane, rows)
        flux = -KAPPA * mask * raw[at]
        for k in range(3):
            flux = flux + scaled[k] * surf[k, f]
        out[at] = out[at] + flux
    for copy in sends + surf_sends:
        copy.wait_send()


def shards(n_lat, n_lon, state, push, fill, vertical, land, match, counts):
    _, fields, levels, rows, cols = state.shape
    assert fields == 3 and 8 * rows <= cols
    block = (rows, levels, cols)
    side = (STEPS, levels, cols)
    n_sems = 3 + 4 * STEPS + 9
    f32 = jnp.float32
    any_spec = pl.BlockSpec(memory_space=pl.ANY)
    result = pl.pallas_call(
        functools.partial(kernel, (levels, rows, cols, n_lat, n_lon)),
        out_shape=jax.ShapeDtypeStruct((fields * levels * rows, cols), f32),
        in_specs=[any_spec] * 7,
        out_specs=pl.BlockSpec(memory_space=pltpu.VMEM),
        scratch_shapes=[
            pltpu.VMEM((fields * levels * rows, cols), f32),
            pltpu.VMEM(push.shape, f32),
            pltpu.VMEM(fill.shape, f32),
            pltpu.VMEM(vertical.shape[1:], f32),
            pltpu.VMEM(land.shape, jnp.int32),
            pltpu.VMEM(match.shape[1:], jnp.int32),
            pltpu.VMEM(counts.shape[1:], jnp.int32),
            pltpu.VMEM(block, f32),
            pltpu.VMEM(block, f32),
            pltpu.VMEM(block, f32),
            pltpu.VMEM(block, f32),
            pltpu.VMEM(block, f32),
            pltpu.VMEM(block, f32),
            pltpu.VMEM(side, f32),
            pltpu.VMEM(side, f32),
            pltpu.VMEM(side, f32),
            pltpu.VMEM((STEPS, 2, 2, levels, cols), f32),
            pltpu.VMEM((STEPS, 2, levels, cols), f32),
            pltpu.VMEM((STEPS, 2, levels, cols), f32),
            pltpu.VMEM((3, fields, rows, cols), f32),
            pltpu.SemaphoreType.DMA((9,)),
            pltpu.SemaphoreType.DMA((n_sems,)),
            pltpu.SemaphoreType.DMA((n_sems,)),
        ],
        compiler_params=pltpu.CompilerParams(collective_id=0, has_side_effects=True),
        name="window",
    )(
        state.reshape(fields * levels * rows, cols),
        push,
        fill,
        vertical.reshape(vertical.shape[1:]),
        land,
        match.reshape(match.shape[1:]),
        counts.reshape(counts.shape[1:]),
    )
    return result.reshape(state.shape)


def solution(mesh):
    sizes = dict(mesh.shape)
    return jax.shard_map(
        functools.partial(shards, sizes["lat"], sizes["lon"]),
        mesh=mesh,
        in_specs=(
            P("comp", None, None, "lat", "lon"),
            P("comp", None),
            P("comp", None),
            P("comp", None, None),
            P("lat", "lon"),
            P("lat", None, None),
            P("lat", None, None),
        ),
        out_specs=P("comp", None, None, "lat", "lon"),
        check_vma=False,
    )
```

time: 48.7 us -> 20.5 us (0.42)
  Pallas kernels: 0 us -> 16.2 us
  starting transfers between devices: 15.7 us -> 0 us
  other arithmetic: 11 us -> 0 us
  local copies, waits for them, and re-layouts: 11 us -> 4.07 us
  waiting for transfers between devices: 6.07 us -> 0 us
  between operations: 3.4 us -> 0.01 us
  matrix products: 1.16 us -> 0 us
    pallas_call x0 -> x1, Pallas kernels: none -> 16.2 us  [shards(): pl.pallas_call(functools.partial(kernel, (levels, rows, cols, n_lat, n_lo...]
    ppermute x11 -> x0, starting transfers between devices: 15.7 us -> none  [the longest x4 8.9 us: extended_2(): lax.ppermute(lax.slice_in_dim(block, 0, width, axis=dim), axis, backward)]
    ppermute x11 -> x0, waiting for transfers between devices: 6.07 us -> none  [the longest x4 3.8 us: extended_2(): lax.ppermute(lax.slice_in_dim(block, block.shape[dim] - width, None, axis...]
    mul x8 -> x0, other arithmetic: 4.07 us -> none  [the longest x2 2.06 us: shards(): extended = extended * valid[None, None, :, None]]
    slice x12 -> x0, local copies, waits for them, and re-layouts: 3.81 us -> none  [the longest x5 2.33 us: extended_2(): lax.slice_in_dim(block, block.shape[dim] - width, None, axis=dim)]
    concatenate x3 -> x0, other arithmetic: 2.9 us -> none  [extended_2(): block = jnp.concatenate([low, block, high], axis=dim)]
    ppermute x4 -> x0, local copies, waits for them, and re-layouts: 2.82 us -> none  [the longest x2 1.82 us: extended_2(): lax.ppermute(lax.slice_in_dim(block, 0, width, axis=dim), axis, backward)]
    add x1 -> x0, other arithmetic: 1.46 us -> none  [shards(): top = current[:, 0] + flux]
  transfers between devices with their start and end apart: 11 -> 0, of which waited for: 5 -> 0; matrix products, arithmetic and copies ran while one was open for 27% -> 0% of each run, Pallas kernels for 0% -> 0%
where the time goes in v1:
time: 20.5 us; the launch traced here: 20.3 us
  Pallas kernels  16.2 us (79%)
  local copies, waits for them, and re-layouts  4.07 us (20%)
    pallas_call x1, Pallas kernels, shards(): pl.pallas_call(functools.partial(kernel, (levels, rows, cols, n_lat, n_lo...  16.2 us
    unnamed x5, local copies, waits for them, and re-layouts  2.76 us
    reshape x1, local copies, waits for them, and re-layouts, shards(): match.reshape(match.shape[1:])  0.66 us
    reshape x1, local copies, waits for them, and re-layouts, shards(): counts.reshape(counts.shape[1:])  0.65 us

profile of v1, /device:TPU:0, one launch (start us, length us, event | category | flops | bytes accessed | tf_op | source)
XLA Modules:
  0.0 20.3 jit_solution(9616297030757110927)
XLA Ops:
  0.0 0.0 copy-start
  0.0 0.7 %copy-done = s32[1,4,2]{1,2,0:T(2,128)S(1)} copy-done((s32[1,4,2]{1,2,0:T(2,128)S(1)}, s32[1,4,2]{1,2,0:T(2,128)}, u32[]{:S(2)}) %copy-start) | copy-done | bytes 56
  0.7 0.0 copy-start.1
  0.7 0.7 %copy.8.match_in = s32[4,2]{1,0:T(4,128)} copy(s32[4,2]{0,1:T(2,128)S(1)} %bitcast.8) | data formatting | bytes 64 | tf_op jit(solution)/shard_map/reshape | solution.py:347
  1.3 0.0 copy-done.1
  1.4 0.6 %copy.9.count_in = s32[4,2]{1,0:T(4,128)} copy(s32[4,2]{0,1:T(2,128)S(1)} %bitcast.9) | data formatting | bytes 64 | tf_op jit(solution)/shard_map/reshape | solution.py:348
  2.0 16.2 %window.1 = f32[1536,128]{1,0:T(8,128)} custom-call(f32[1536,128]{1,0:T(8,128)} %bitcast.6, f32[1,32]{1,0:T(1,128)} %push_in.1, f32[1,32]{1,0:T(1,128)} %fill_in.1, f32[32,32]{1,0:T(8,128)} %bitcast.7, s32[16,128]{1,0:T(8,128)} %land_in.1, s32[4,2]{1,0:T(4,128)} %copy.8.match_in, s32[4,2]{1,0:T(4,128)} %copy.9.count_in), custom_call_target="tpu_custom_call" | custom-call | tf_op jit(solution)/shard_map/window/pallas_call | solution.py:309
  18.2 2.1 %copy.11 = f32[1,3,32,16,128]{4,3,2,1,0:T(8,128)} copy(f32[1,3,32,16,128]{4,3,2,1,0:T(8,128)} %bitcast.5) | data formatting | bytes 1572864
Async XLA Ops:
  0.0 0.7 %copy-start = (s32[1,4,2]{1,2,0:T(2,128)S(1)}, s32[1,4,2]{1,2,0:T(2,128)}, u32[]{:S(2)}) copy-start(s32[1,4,2]{1,2,0:T(2,128)} %param.12) | copy-start | bytes 100
  0.7 0.7 %copy-start.1 = (s32[1,4,2]{1,2,0:T(2,128)S(1)}, s32[1,4,2]{1,2,0:T(2,128)}, u32[]{:S(2)}) copy-start(s32[1,4,2]{1,2,0:T(2,128)} %param.13) | copy-start | bytes 100

commit v2 on v1

--- a/solution.py
+++ b/solution.py
@@ -274,7 +274,7 @@
 
     count = count_v[...].astype(jnp.float32)
     match = match_v[...]
-    tile = lax.broadcasted_iota(jnp.int32, match.shape, 0)
+    tile = lax.broadcasted_iota(jnp.int32, match.shape, 1)
 
     def coef(peer):
         own = jnp.where((tile == lon) & (match == peer), count, 0.0)
@@ -308,7 +308,7 @@
     any_spec = pl.BlockSpec(memory_space=pl.ANY)
     result = pl.pallas_call(
         functools.partial(kernel, (levels, rows, cols, n_lat, n_lon)),
-        out_shape=jax.ShapeDtypeStruct((fields * levels * rows, cols), f32),
+        out_shape=pltpu.VMEM((fields * levels * rows, cols), f32),
         in_specs=[any_spec] * 7,
         out_specs=pl.BlockSpec(memory_space=pltpu.VMEM),
         scratch_shapes=[
@@ -317,8 +317,8 @@
             pltpu.VMEM(fill.shape, f32),
             pltpu.VMEM(vertical.shape[1:], f32),
             pltpu.VMEM(land.shape, jnp.int32),
-            pltpu.VMEM(match.shape[1:], jnp.int32),
-            pltpu.VMEM(counts.shape[1:], jnp.int32),
+            pltpu.VMEM(match.shape[:0:-1], jnp.int32),
+            pltpu.VMEM(counts.shape[:0:-1], jnp.int32),
             pltpu.VMEM(block, f32),
             pltpu.VMEM(block, f32),
             pltpu.VMEM(block, f32),
@@ -344,8 +344,8 @@
         fill,
         vertical.reshape(vertical.shape[1:]),
         land,
-        match.reshape(match.shape[1:]),
-        counts.reshape(counts.shape[1:]),
+        match[0].T,
+        counts[0].T,
     )
     return result.reshape(state.shape)
 

time: 20.5 us -> 16.4 us (0.80)
  local copies, waits for them, and re-layouts: 4.07 us -> 0.88 us
  Pallas kernels: 16.2 us -> 15.3 us
    unnamed x5 -> x1, local copies, waits for them, and re-layouts: 2.76 us -> 0.88 us
    reshape x2 -> x0, local copies, waits for them, and re-layouts: 1.31 us -> none  [the longest x1 0.66 us: shards(): match.reshape(match.shape[1:])]
    pallas_call x1, Pallas kernels: 16.2 us -> 15.3 us  [shards(): pl.pallas_call(functools.partial(kernel, (levels, rows, cols, n_lat, n_lo...]
where the time goes in v2:
time: 16.4 us; the launch traced here: 16.2 us
  Pallas kernels  15.3 us (93%)
  local copies, waits for them, and re-layouts  0.88 us (5%)
    pallas_call x1, Pallas kernels, shards(): pl.pallas_call(functools.partial(kernel, (levels, rows, cols, n_lat, n_lo...  15.3 us
    unnamed x1, local copies, waits for them, and re-layouts  0.88 us

profile of v2, /device:TPU:0, one launch (start us, length us, event | category | flops | bytes accessed | tf_op | source)
XLA Modules:
  0.0 16.2 jit_solution(4524267898006980724)
XLA Ops:
  0.0 15.3 %window.1 = f32[1536,128]{1,0:T(8,128)S(1)} custom-call(f32[1536,128]{1,0:T(8,128)} %bitcast.10, f32[1,32]{1,0:T(1,128)} %push_in.1, f32[1,32]{1,0:T(1,128)} %fill_in.1, f32[32,32]{1,0:T(8,128)} %bitcast.11, s32[16,128]{1,0:T(8,128)} %land_in.1, s32[2,4]{1,0:T(2,128)} %bitcast.12, s32[2,4]{1,0:T(2,128)} %bitcast.13), custom_call_target="tpu_custom_call" | custom-call | tf_op jit(solution)/shard_map/window/pallas_call | solution.py:309
  15.3 0.9 %copy.9 = f32[1,3,32,16,128]{4,3,2,1,0:T(8,128)} copy(f32[1,3,32,16,128]{4,3,2,1,0:T(8,128)S(1)} %bitcast.9) | data formatting | bytes 1572864

commit v3 on v2

--- a/solution.py
+++ b/solution.py
@@ -134,6 +134,31 @@
     def ahead(x):
         return jnp.where(last, 0.0, pltpu.roll(x, cols - 1, 1))
 
+    spread = jnp.broadcast_to
+    groups = levels // 8
+    lane8 = lane[:8]
+    side_angle = ((lane8 // 4 + lat * rows).astype(jnp.float32) + 0.5) / (n_lat * rows) - 0.5
+    side_fcor = CORIOLIS * jnp.sin(math.pi * side_angle)
+    side_fcor = jnp.concatenate([side_fcor] * groups, axis=0)
+    owner = lane // 4
+
+    def gather(take):
+        first_row = take(0)
+        result = jnp.zeros_like(first_row)
+        for y in range(rows):
+            value = first_row if y == 0 else take(y)
+            turned = pltpu.roll(value, 4 * y + 2, 1)
+            result = jnp.where(owner[: value.shape[0]] == y, turned, result)
+        return result
+
+    side_mask = gather(lambda y: spread(mask[y : y + 1], (8, cols)))
+    side_mask = jnp.concatenate([side_mask] * groups, axis=0)
+
+    def split(x):
+        hi = x.astype(jnp.bfloat16)
+        lo = (x - hi.astype(jnp.float32)).astype(jnp.bfloat16)
+        return jnp.concatenate([hi, lo, hi], axis=0)
+
     def remote(src, dst, k, to):
         return pltpu.make_async_remote_copy(
             src_ref=src,
@@ -146,28 +171,50 @@
 
     sends = []
     surf_sends = []
+
+    def send_sides(step, p_side, u_side, v_side):
+        inner = jnp.where(quad == 1, pltpu.roll(p_side, 1, 1), -pltpu.roll(p_side, cols - 1, 1))
+        w_side = u_side + side_fcor * v_side + hp * inner
+        packed = jnp.where(lane < 4 * rows, p_side, pltpu.roll(w_side, 4 * rows, 1))
+        for k in (0, 1):
+            dense = jnp.zeros((8, cols), jnp.float32)
+            for g in range(groups):
+                turn = (g - 1 - k) % cols
+                part = packed[8 * g : 8 * g + 8]
+                part = pltpu.roll(part, turn, 1) if turn else part
+                dense = jnp.where(quad[:8] == g, part, dense)
+            pack[step, k] = dense
+        if step == 0:
+            pl.semaphore_wait(barrier, 7)
+        base = 3 + 4 * step
+        lo = remote(pack.at[step, 0], from_lo.at[step], base, (comp, lat, east))
+        hi = remote(pack.at[step, 1], from_hi.at[step], base + 1, (comp, lat, west))
+        for copy in (hi, lo):
+            copy.start()
+            sends.append(copy)
+        return packed, lo, hi
+
+    def raw_row(f, y):
+        return raw[pl.ds(f * plane + y, levels, stride=rows), :]
+
+    def first_p(y):
+        p = raw_row(2, y)
+        pres[y] = p
+        return p
+
+    side = send_sides(
+        0,
+        gather(first_p),
+        gather(functools.partial(raw_row, 0)),
+        gather(functools.partial(raw_row, 1)),
+    )
     for step in range(STEPS):
         base = 3 + 4 * step
+        packed, lo, hi = side
 
         def get(f, y):
-            if step == 0:
-                return raw[pl.ds(f * plane + y, levels, stride=rows), :]
-            return (unew, vnew, pres)[f][y]
-
-        packed = jnp.zeros((levels, cols), jnp.float32)
-        for y in range(rows):
-            p = get(2, y)
-            if step == 0:
-                pres[y] = p
-            u1 = get(0, y) + fcor[y : y + 1] * get(1, y) - hp * (ahead(p) - back(p))
-            uone[y] = u1
-            at = 4 * y + 2
-            here = (lane == at) | (lane == at - 1)
-            packed = jnp.where(here, pltpu.roll(p, at, 1), packed)
-            at = 4 * (rows + y) + 2
-            here = (lane == at) | (lane == at - 1)
-            packed = jnp.where(here, pltpu.roll(u1, at, 1), packed)
-        pack[step] = packed
+            return raw_row(f, y) if step == 0 else (unew, vnew, pres)[f][y]
+
         for y in (0, rows - 1):
             v1 = get(1, y) - fcor[y : y + 1] * get(0, y)
             v1 = v1 - hp * pres[y + 1] if y == 0 else v1 + hp * pres[y - 1]
@@ -175,13 +222,9 @@
             k = 0 if y == 0 else 1
             edge[step, k, 0] = pres[y]
             edge[step, k, 1] = v1
-        if step == 0:
-            pl.semaphore_wait(barrier, 7)
-        lo = remote(pack.at[step], from_lo.at[step], base, (comp, lat, east))
-        hi = remote(pack.at[step], from_hi.at[step], base + 1, (comp, lat, west))
         down = remote(edge.at[step, 0], row_hi.at[step], base + 2, (comp, south, lon))
         up = remote(edge.at[step, 1], row_lo.at[step], base + 3, (comp, north, lon))
-        for copy in (lo, hi, down, up):
+        for copy in (down, up):
             copy.start()
             sends.append(copy)
         if step == 0:
@@ -200,6 +243,9 @@
             vone[y] = (
                 get(1, y) - fcor[y : y + 1] * get(0, y) - hp * (pres[y + 1] - pres[y - 1])
             )
+        for y in range(rows):
+            p = pres[y]
+            uone[y] = get(0, y) + fcor[y : y + 1] * get(1, y) - hp * (ahead(p) - back(p))
         for y in range(rows):
             u1 = uone[y]
             div = ahead(u1) - back(u1)
@@ -224,13 +270,20 @@
         pone[rows - 1] = pone[rows - 1] - hf * v_hi
         pone[rows - 2] = pone[rows - 2] - hf * fix_hi
 
+        if step + 1 < STEPS:
+            p_side = gather(lambda y: pone[y])
+            u_edge = gather(lambda y: uone[y])
+            v_edge = gather(lambda y: vone[y])
         lo.wait_recv()
         hi.wait_recv()
-        moved = jnp.where(
-            quad == 1,
-            pltpu.roll(from_hi[step], cols - 1, 1),
-            pltpu.roll(from_lo[step], 1, 1),
-        )
+        moved = []
+        for g in range(groups):
+            low, high = (
+                pltpu.roll(box[step], turn % cols, 1) if turn else box[step]
+                for box, turn in ((from_lo, 2 - g), (from_hi, 1 - g))
+            )
+            moved.append(jnp.where(quad[:8] == 1, high, low))
+        moved = jnp.concatenate(moved, axis=0)
         signed = jnp.where(quad == 1, hp, -hp)
         u_side = pltpu.roll(moved, cols - 4 * rows, 1) + signed * packed
         u_fix = -signed * moved
@@ -248,14 +301,22 @@
         d_fix = hf * d_fix
         ends = first | last
         near = (lane < 2) | (lane > cols - 3)
+        if step + 1 < STEPS:
+            p_side = jnp.dot(
+                vert_cat, split(p_side - d_fix), preferred_element_type=jnp.float32
+            )
+            side = send_sides(
+                step + 1,
+                side_mask * p_side,
+                side_mask * (u_edge + u_fix),
+                side_mask * v_edge,
+            )
         pieces = []
         for y in range(rows):
             turn = cols - (4 * y + 2)
             uone[y] = uone[y] + jnp.where(ends, pltpu.roll(u_fix, turn, 1), 0.0)
             p1 = pone[y] - jnp.where(near, pltpu.roll(d_fix, turn, 1), 0.0)
-            p1_hi = p1.astype(jnp.bfloat16)
-            p1_lo = (p1 - p1_hi.astype(jnp.float32)).astype(jnp.bfloat16)
-            pieces.append(jnp.concatenate([p1_hi, p1_lo, p1_hi], axis=0))
+            pieces.append(split(p1))
         p2 = jnp.dot(
             vert_cat, jnp.concatenate(pieces, axis=1), preferred_element_type=jnp.float32
         )
@@ -300,9 +361,8 @@
 
 def shards(n_lat, n_lon, state, push, fill, vertical, land, match, counts):
     _, fields, levels, rows, cols = state.shape
-    assert fields == 3 and 8 * rows <= cols
+    assert fields == 3 and 8 * rows <= cols and levels % 8 == 0 and levels <= 32
     block = (rows, levels, cols)
-    side = (STEPS, levels, cols)
     n_sems = 3 + 4 * STEPS + 9
     f32 = jnp.float32
     any_spec = pl.BlockSpec(memory_space=pl.ANY)
@@ -325,9 +385,9 @@
             pltpu.VMEM(block, f32),
             pltpu.VMEM(block, f32),
             pltpu.VMEM(block, f32),
-            pltpu.VMEM(side, f32),
-            pltpu.VMEM(side, f32),
-            pltpu.VMEM(side, f32),
+            pltpu.VMEM((STEPS, 2, 8, cols), f32),
+            pltpu.VMEM((STEPS, 8, cols), f32),
+            pltpu.VMEM((STEPS, 8, cols), f32),
             pltpu.VMEM((STEPS, 2, 2, levels, cols), f32),
             pltpu.VMEM((STEPS, 2, levels, cols), f32),
             pltpu.VMEM((STEPS, 2, levels, cols), f32),

time: 16.4 us -> 15.7 us (0.957)
  Pallas kernels: 15.3 us -> 14.7 us
    pallas_call x1, Pallas kernels: 15.3 us -> 14.7 us  [shards(): pl.pallas_call(functools.partial(kernel, (levels, rows, cols, n_lat, n_lo...]
where the time goes in v3:
time: 15.7 us; the launch traced here: 15.6 us
  Pallas kernels  14.7 us (94%)
  local copies, waits for them, and re-layouts  0.88 us (6%)
    pallas_call x1, Pallas kernels, shards(): pl.pallas_call(functools.partial(kernel, (levels, rows, cols, n_lat, n_lo...  14.7 us
    unnamed x1, local copies, waits for them, and re-layouts  0.88 us

profile of v3, /device:TPU:0, one launch (start us, length us, event | category | flops | bytes accessed | tf_op | source)
XLA Modules:
  0.0 15.6 jit_solution(5692871857644681421)
XLA Ops:
  0.0 14.7 %window.1 = f32[1536,128]{1,0:T(8,128)S(1)} custom-call(f32[1536,128]{1,0:T(8,128)} %bitcast.10, f32[1,32]{1,0:T(1,128)} %push_in.1, f32[1,32]{1,0:T(1,128)} %fill_in.1, f32[32,32]{1,0:T(8,128)} %bitcast.11, s32[16,128]{1,0:T(8,128)} %land_in.1, s32[2,4]{1,0:T(2,128)} %bitcast.12, s32[2,4]{1,0:T(2,128)} %bitcast.13), custom_call_target="tpu_custom_call" | custom-call | tf_op jit(solution)/shard_map/window/pallas_call | solution.py:369
  14.7 0.9 %copy.9 = f32[1,3,32,16,128]{4,3,2,1,0:T(8,128)} copy(f32[1,3,32,16,128]{4,3,2,1,0:T(8,128)S(1)} %bitcast.9) | data formatting | bytes 1572864

commit v4 on v3

--- a/solution.py
+++ b/solution.py
@@ -208,6 +208,30 @@
         gather(functools.partial(raw_row, 0)),
         gather(functools.partial(raw_row, 1)),
     )
+    def add_flux():
+        count = count_v[...].astype(jnp.float32)
+        match = match_v[...]
+        tile = lax.broadcasted_iota(jnp.int32, match.shape, 1)
+
+        def coef(peer):
+            own = jnp.where((tile == lon) & (match == peer), count, 0.0)
+            theirs = jnp.where((tile == peer) & (match == lon), count, 0.0)
+            picked = jnp.where(comp == 1, own, theirs)
+            total = jnp.sum(jnp.sum(picked, axis=1, keepdims=True), axis=0, keepdims=True)
+            return jnp.broadcast_to(total, (rows, cols))
+
+        coefs = [coef(lon), coef(west), coef(east)]
+        inverse = KAPPA * mask / (coefs[0] + coefs[1] + coefs[2])
+        scaled = [c * inverse for c in coefs]
+        for copy in surf_sends:
+            copy.wait_recv()
+        for f in range(3):
+            at = pl.ds(f * plane, rows)
+            flux = -KAPPA * mask * raw[at]
+            for k in range(3):
+                flux = flux + scaled[k] * surf[k, f]
+            out[at] = out[at] + flux
+
     for step in range(STEPS):
         base = 3 + 4 * step
         packed, lo, hi = side
@@ -274,6 +298,18 @@
             p_side = gather(lambda y: pone[y])
             u_edge = gather(lambda y: uone[y])
             v_edge = gather(lambda y: vone[y])
+        else:
+            p2 = jnp.dot(
+                vert_cat,
+                jnp.concatenate([split(pone[y]) for y in range(rows)], axis=1),
+                preferred_element_type=jnp.float32,
+            )
+            for y in range(rows):
+                keep = mask[y : y + 1]
+                pn = p2[:, y * cols : (y + 1) * cols]
+                for f, value in enumerate((uone[y], vone[y], pn)):
+                    out[pl.ds(f * plane + y, levels, stride=rows), :] = keep * value
+            add_flux()
         lo.wait_recv()
         hi.wait_recv()
         moved = []
@@ -301,16 +337,24 @@
         d_fix = hf * d_fix
         ends = first | last
         near = (lane < 2) | (lane > cols - 3)
-        if step + 1 < STEPS:
-            p_side = jnp.dot(
-                vert_cat, split(p_side - d_fix), preferred_element_type=jnp.float32
+        if step + 1 == STEPS:
+            p_fix = -side_mask * jnp.dot(
+                vert_cat, split(d_fix), preferred_element_type=jnp.float32
             )
-            side = send_sides(
-                step + 1,
-                side_mask * p_side,
-                side_mask * (u_edge + u_fix),
-                side_mask * v_edge,
-            )
+            u_fix = side_mask * u_fix
+            for y in range(rows):
+                turn = cols - (4 * y + 2)
+                for f, fix, where in ((0, u_fix, ends), (2, p_fix, near)):
+                    at = pl.ds(f * plane + y, levels, stride=rows)
+                    out[at, :] = out[at, :] + jnp.where(where, pltpu.roll(fix, turn, 1), 0.0)
+            break
+        p_side = jnp.dot(vert_cat, split(p_side - d_fix), preferred_element_type=jnp.float32)
+        side = send_sides(
+            step + 1,
+            side_mask * p_side,
+            side_mask * (u_edge + u_fix),
+            side_mask * v_edge,
+        )
         pieces = []
         for y in range(rows):
             turn = cols - (4 * y + 2)
@@ -322,39 +366,10 @@
         )
         for y in range(rows):
             keep = mask[y : y + 1]
-            u2 = keep * uone[y]
-            v2 = keep * vone[y]
-            pn = keep * p2[:, y * cols : (y + 1) * cols]
-            if step + 1 < STEPS:
-                unew[y] = u2
-                vnew[y] = v2
-                pres[y] = pn
-            else:
-                for f, value in enumerate((u2, v2, pn)):
-                    out[pl.ds(f * plane + y, levels, stride=rows), :] = value
-
-    count = count_v[...].astype(jnp.float32)
-    match = match_v[...]
-    tile = lax.broadcasted_iota(jnp.int32, match.shape, 1)
-
-    def coef(peer):
-        own = jnp.where((tile == lon) & (match == peer), count, 0.0)
-        theirs = jnp.where((tile == peer) & (match == lon), count, 0.0)
-        picked = jnp.where(comp == 1, own, theirs)
-        total = jnp.sum(jnp.sum(picked, axis=1, keepdims=True), axis=0, keepdims=True)
-        return jnp.broadcast_to(total, (rows, cols))
-
-    coefs = [coef(lon), coef(west), coef(east)]
-    inverse = KAPPA * mask / (coefs[0] + coefs[1] + coefs[2])
-    scaled = [c * inverse for c in coefs]
-    for copy in surf_sends:
-        copy.wait_recv()
-    for f in range(3):
-        at = pl.ds(f * plane, rows)
-        flux = -KAPPA * mask * raw[at]
-        for k in range(3):
-            flux = flux + scaled[k] * surf[k, f]
-        out[at] = out[at] + flux
+            unew[y] = keep * uone[y]
+            vnew[y] = keep * vone[y]
+            pres[y] = keep * p2[:, y * cols : (y + 1) * cols]
+
     for copy in sends + surf_sends:
         copy.wait_send()
 

time: 15.7 us -> 15.7 us (level)
  no operation moved by 1% of the time
where the time goes in v4:
time: 15.7 us; the launch traced here: 15.5 us
  Pallas kernels  14.7 us (94%)
  local copies, waits for them, and re-layouts  0.88 us (6%)
    pallas_call x1, Pallas kernels, shards(): pl.pallas_call(functools.partial(kernel, (levels, rows, cols, n_lat, n_lo...  14.7 us
    unnamed x1, local copies, waits for them, and re-layouts  0.88 us

profile of v4, /device:TPU:0, one launch (start us, length us, event | category | flops | bytes accessed | tf_op | source)
XLA Modules:
  0.0 15.5 jit_solution(4357451488946547848)
XLA Ops:
  0.0 14.7 %window.1 = f32[1536,128]{1,0:T(8,128)S(1)} custom-call(f32[1536,128]{1,0:T(8,128)} %bitcast.10, f32[1,32]{1,0:T(1,128)} %push_in.1, f32[1,32]{1,0:T(1,128)} %fill_in.1, f32[32,32]{1,0:T(8,128)} %bitcast.11, s32[16,128]{1,0:T(8,128)} %land_in.1, s32[2,4]{1,0:T(2,128)} %bitcast.12, s32[2,4]{1,0:T(2,128)} %bitcast.13), custom_call_target="tpu_custom_call" | custom-call | tf_op jit(solution)/shard_map/window/pallas_call | solution.py:384
  14.7 0.9 %copy.9 = f32[1,3,32,16,128]{4,3,2,1,0:T(8,128)} copy(f32[1,3,32,16,128]{4,3,2,1,0:T(8,128)S(1)} %bitcast.9) | data formatting | bytes 1572864

commit v5 on v4

--- a/solution.py
+++ b/solution.py
@@ -66,8 +66,6 @@
         (comp, south, lon),
         (comp, north, lon),
         (other, lat, lon),
-        (other, lat, west),
-        (other, lat, east),
     ):
         pl.semaphore_signal(barrier, inc=1, device_id=to, device_id_type=MESH)
 
@@ -171,6 +169,7 @@
 
     sends = []
     surf_sends = []
+    surf_first = []
 
     def send_sides(step, p_side, u_side, v_side):
         inner = jnp.where(quad == 1, pltpu.roll(p_side, 1, 1), -pltpu.roll(p_side, cols - 1, 1))
@@ -185,7 +184,7 @@
                 dense = jnp.where(quad[:8] == g, part, dense)
             pack[step, k] = dense
         if step == 0:
-            pl.semaphore_wait(barrier, 7)
+            pl.semaphore_wait(barrier, 5)
         base = 3 + 4 * step
         lo = remote(pack.at[step, 0], from_lo.at[step], base, (comp, lat, east))
         hi = remote(pack.at[step, 1], from_hi.at[step], base + 1, (comp, lat, west))
@@ -252,16 +251,16 @@
             copy.start()
             sends.append(copy)
         if step == 0:
-            for k, to in enumerate((lon, east, west)):
-                for f in range(3):
-                    copy = remote(
-                        raw.at[pl.ds(f * plane, rows)],
-                        surf.at[k, f],
-                        3 + 4 * STEPS + 3 * k + f,
-                        (other, lat, to),
-                    )
-                    copy.start()
-                    surf_sends.append(copy)
+            for f in range(3):
+                copy = remote(
+                    raw.at[pl.ds(f * plane, rows)],
+                    surf.at[0, f],
+                    3 + 4 * STEPS + f,
+                    (other, lat, lon),
+                )
+                copy.start()
+                sends.append(copy)
+                surf_first.append(copy)
 
         for y in range(1, rows - 1):
             vone[y] = (
@@ -310,6 +309,13 @@
                 for f, value in enumerate((uone[y], vone[y], pn)):
                     out[pl.ds(f * plane + y, levels, stride=rows), :] = keep * value
             add_flux()
+        if step == 0:
+            for copy in surf_first:
+                copy.wait_recv()
+            for k, to in ((1, east), (2, west)):
+                copy = remote(surf.at[0], surf.at[k], 5 + 4 * STEPS + k, (comp, lat, to))
+                copy.start()
+                surf_sends.append(copy)
         lo.wait_recv()
         hi.wait_recv()
         moved = []
@@ -378,7 +384,7 @@
     _, fields, levels, rows, cols = state.shape
     assert fields == 3 and 8 * rows <= cols and levels % 8 == 0 and levels <= 32
     block = (rows, levels, cols)
-    n_sems = 3 + 4 * STEPS + 9
+    n_sems = 3 + 4 * STEPS + 5
     f32 = jnp.float32
     any_spec = pl.BlockSpec(memory_space=pl.ANY)
     result = pl.pallas_call(

time: 15.7 us -> 14.6 us (0.930)
  Pallas kernels: 14.7 us -> 13.6 us
    pallas_call x1, Pallas kernels: 14.7 us -> 13.6 us  [shards(): pl.pallas_call(functools.partial(kernel, (levels, rows, cols, n_lat, n_lo...]
where the time goes in v5:
time: 14.6 us; the launch traced here: 14.5 us
  Pallas kernels  13.6 us (93%)
  local copies, waits for them, and re-layouts  0.88 us (6%)
    pallas_call x1, Pallas kernels, shards(): pl.pallas_call(functools.partial(kernel, (levels, rows, cols, n_lat, n_lo...  13.6 us
    unnamed x1, local copies, waits for them, and re-layouts  0.88 us

profile of v5, /device:TPU:0, one launch (start us, length us, event | category | flops | bytes accessed | tf_op | source)
XLA Modules:
  0.0 14.5 jit_solution(4903378895306265436)
XLA Ops:
  0.0 13.6 %window.1 = f32[1536,128]{1,0:T(8,128)S(1)} custom-call(f32[1536,128]{1,0:T(8,128)} %bitcast.10, f32[1,32]{1,0:T(1,128)} %push_in.1, f32[1,32]{1,0:T(1,128)} %fill_in.1, f32[32,32]{1,0:T(8,128)} %bitcast.11, s32[16,128]{1,0:T(8,128)} %land_in.1, s32[2,4]{1,0:T(2,128)} %bitcast.12, s32[2,4]{1,0:T(2,128)} %bitcast.13), custom_call_target="tpu_custom_call" | custom-call | tf_op jit(solution)/shard_map/window/pallas_call | solution.py:390
  13.6 0.9 %copy.9 = f32[1,3,32,16,128]{4,3,2,1,0:T(8,128)} copy(f32[1,3,32,16,128]{4,3,2,1,0:T(8,128)S(1)} %bitcast.9) | data formatting | bytes 1572864

commit v6 on v5

--- a/solution.py
+++ b/solution.py
@@ -174,13 +174,14 @@
     def send_sides(step, p_side, u_side, v_side):
         inner = jnp.where(quad == 1, pltpu.roll(p_side, 1, 1), -pltpu.roll(p_side, cols - 1, 1))
         w_side = u_side + side_fcor * v_side + hp * inner
-        packed = jnp.where(lane < 4 * rows, p_side, pltpu.roll(w_side, 4 * rows, 1))
         for k in (0, 1):
             dense = jnp.zeros((8, cols), jnp.float32)
             for g in range(groups):
-                turn = (g - 1 - k) % cols
-                part = packed[8 * g : 8 * g + 8]
-                part = pltpu.roll(part, turn, 1) if turn else part
+                turn = g - 1 - k
+                p_part = p_side[8 * g : 8 * g + 8]
+                p_part = pltpu.roll(p_part, turn % cols, 1) if turn else p_part
+                w_part = pltpu.roll(w_side[8 * g : 8 * g + 8], 4 * rows + turn, 1)
+                part = jnp.where(lane8 < 4 * rows, p_part, w_part)
                 dense = jnp.where(quad[:8] == g, part, dense)
             pack[step, k] = dense
         if step == 0:
@@ -191,7 +192,7 @@
         for copy in (hi, lo):
             copy.start()
             sends.append(copy)
-        return packed, lo, hi
+        return p_side, lo, hi
 
     def raw_row(f, y):
         return raw[pl.ds(f * plane + y, levels, stride=rows), :]
@@ -318,16 +319,20 @@
                 surf_sends.append(copy)
         lo.wait_recv()
         hi.wait_recv()
-        moved = []
-        for g in range(groups):
-            low, high = (
-                pltpu.roll(box[step], turn % cols, 1) if turn else box[step]
-                for box, turn in ((from_lo, 2 - g), (from_hi, 1 - g))
-            )
-            moved.append(jnp.where(quad[:8] == 1, high, low))
-        moved = jnp.concatenate(moved, axis=0)
+
+        def unpack(offset):
+            parts = []
+            for g in range(groups):
+                low, high = (
+                    pltpu.roll(box[step], turn % cols, 1) if turn % cols else box[step]
+                    for box, turn in ((from_lo, offset + 2 - g), (from_hi, offset + 1 - g))
+                )
+                parts.append(jnp.where(quad[:8] == 1, high, low))
+            return jnp.concatenate(parts, axis=0)
+
+        moved = unpack(0)
         signed = jnp.where(quad == 1, hp, -hp)
-        u_side = pltpu.roll(moved, cols - 4 * rows, 1) + signed * packed
+        u_side = unpack(cols - 4 * rows) + signed * packed
         u_fix = -signed * moved
         d_fix = jnp.where(
             quad == 1,

time: 14.6 us -> 14.5 us (level)
  Pallas kernels: 13.6 us -> 13.4 us
    pallas_call x1, Pallas kernels: 13.6 us -> 13.4 us  [shards(): pl.pallas_call(functools.partial(kernel, (levels, rows, cols, n_lat, n_lo...]
where the time goes in v6:
time: 14.5 us; the launch traced here: 14.3 us
  Pallas kernels  13.4 us (92%)
  local copies, waits for them, and re-layouts  0.88 us (6%)
    pallas_call x1, Pallas kernels, shards(): pl.pallas_call(functools.partial(kernel, (levels, rows, cols, n_lat, n_lo...  13.4 us
    unnamed x1, local copies, waits for them, and re-layouts  0.88 us

profile of v6, /device:TPU:0, one launch (start us, length us, event | category | flops | bytes accessed | tf_op | source)
XLA Modules:
  0.0 14.3 jit_solution(17847242930679060669)
XLA Ops:
  0.0 13.4 %window.1 = f32[1536,128]{1,0:T(8,128)S(1)} custom-call(f32[1536,128]{1,0:T(8,128)} %bitcast.10, f32[1,32]{1,0:T(1,128)} %push_in.1, f32[1,32]{1,0:T(1,128)} %fill_in.1, f32[32,32]{1,0:T(8,128)} %bitcast.11, s32[16,128]{1,0:T(8,128)} %land_in.1, s32[2,4]{1,0:T(2,128)} %bitcast.12, s32[2,4]{1,0:T(2,128)} %bitcast.13), custom_call_target="tpu_custom_call" | custom-call | tf_op jit(solution)/shard_map/window/pallas_call | solution.py:395
  13.4 0.9 %copy.9 = f32[1,3,32,16,128]{4,3,2,1,0:T(8,128)} copy(f32[1,3,32,16,128]{4,3,2,1,0:T(8,128)S(1)} %bitcast.9) | data formatting | bytes 1572864
